TPU v7x, 128 devices: a whole 4x4x4 slice. The times are simulated.
128 devices in a mesh: lon: 16 (over y_lo, x, core), lat: 8 (over z, y_hi).
Axes of the slice: x: 4, y: 4 (y_hi: 2, y_lo: 2; y = y_hi * 2 + y_lo), z: 4, core: 2. Of those that a mesh axis runs over, the one named last changes fastest.
Arguments:
- courant_east: float32 [72, 512, 2048], P(None, 'lat', 'lon'), may hold values from -0.4 to 0.4
- courant_north: float32 [72, 512, 2048], P(None, 'lat', 'lon'), may hold values from -0.4 to 0.4
- obs_cells: int32 [8, 16, 1024], P('lat', 'lon'), may hold values from 0 to 8191
- misfit: float32 [5, 8, 16, 1024], P(None, 'lat', 'lon'), may hold values from -6 to 6
- kernel: float32 [72], replicated, may hold values from 0.25 to 1.75
- ensemble: bfloat16 [64, 512, 2048], P(None, 'lat', 'lon'), may hold values from -0.75 to 0.75
- pair_src: int32 [131072], P(('lon', 'lat')), may hold values from 0 to 4095
- pair_dst: int32 [131072], P(('lon', 'lat')), may hold values from 0 to 4095, as said below
- taper: float32 [131072], P(('lon', 'lat')), may hold values from 0.1 to 1
- var_scale: float32 [512, 2048], P('lat', 'lon'), may hold values from 0.3 to 3
Outputs:
- adjoint_field: float32 [72, 512, 2048], P(None, 'lat', 'lon')
- prior_grad: float32 [512, 2048], P('lat', 'lon')
Inputs may be any that keep to these rules, and one draw needn't show every extreme that they name: `obs_cells`: each index names a cell of its own tile. `pair_dst`: block numbers; among the 1024 pairs of one device at most 64 name blocks of one tile, and some tile gets exactly 64 of them.
All inputs are finite; a program needn't handle non-finite values.
Results may differ from a plain program's by a relative error of at most 0.004.
Values sent between devices are 32-bit elements; how exact they have to be, the bound alone decides.
A program may use at most 128 MiB of HBM per device.

v0:
```python
import jax
import jax.numpy as jnp
from jax import lax
from jax.sharding import PartitionSpec as P

BLK = 16


def passed_along(block, axis, distance):
    devices = range(lax.axis_size(axis))
    route = [((i - distance) % len(devices), i) for i in devices]
    return lax.ppermute(block, axis, route)


def from_behind(value, axis, steps):
    count = lax.axis_size(axis)
    initial, last = (max(0, -steps), min(count, count - steps))
    return lax.ppermute(value, axis, [(source, source + steps) for source in range(initial, last)])


def with_halo(block, sides, width):
    for axis, dim in sides:
        count = lax.axis_size(axis)
        forward = [(i, i + 1) for i in range(count - 1)]
        forward.append((count - 1, 0))
        backward = [(target, source) for source, target in forward]
        low = lax.ppermute(
            lax.slice_in_dim(block, block.shape[dim] - width, None, axis=dim), axis, forward
        )
        high = lax.ppermute(lax.slice_in_dim(block, 0, width, axis=dim), axis, backward)
        block = jnp.concatenate([low, block, high], axis=dim)
    return block


def per_device(
    courant_east,
    courant_north,
    obs_cells,
    misfit,
    kernel,
    ensemble,
    pair_src,
    pair_dst,
    taper,
    var_scale,
):
    levels, tile_lat, tile_lon = courant_east.shape
    lat_count = lax.axis_size("lat")
    lon_count = lax.axis_size("lon")
    rows_global = lax.axis_index("lat") * tile_lat + jnp.arange(tile_lat, dtype=jnp.int32)
    keep_rows = (rows_global < tile_lat * lat_count - 1)[None, :, None]
    north_face = jnp.where(keep_rows, courant_north, 0.0)
    pos_east = jnp.maximum(courant_east, 0.0)
    pos_north = jnp.maximum(north_face, 0.0)
    neg_east = jnp.minimum(courant_east, 0.0)
    neg_north = jnp.minimum(north_face, 0.0)
    west_column = passed_along(neg_east[:, :, -1:], "lon", 1)
    neg_west = jnp.concatenate([west_column, neg_east[:, :, :-1]], axis=2)
    south_row = from_behind(neg_north[:, -1:, :], "lat", 1)
    neg_south = jnp.concatenate([south_row, neg_north[:, :-1, :]], axis=1)
    flat_cells = obs_cells.reshape(-1)

    def forcing(step_index):
        column = (
            jnp.zeros((tile_lat * tile_lon,), jnp.float32)
            .at[flat_cells]
            .add(misfit[step_index].reshape(-1))
        )
        return kernel[:, None, None] * column.reshape(tile_lat, tile_lon)[None]

    adj_field = forcing(0)
    surface = adj_field[0]
    for step_index in range(1, misfit.shape[0]):
        padded = with_halo(adj_field, (("lat", 1), ("lon", 2)), 1)
        east_vals = padded[:, 1:-1, 2:]
        west_vals = padded[:, 1:-1, :-2]
        north_vals = padded[:, 2:, 1:-1]
        south_vals = padded[:, :-2, 1:-1]
        adj_field = (
            adj_field
            + pos_east * (east_vals - adj_field)
            + neg_west * (adj_field - west_vals)
            + pos_north * (north_vals - adj_field)
            + neg_south * (adj_field - south_vals)
            + forcing(step_index)
        )
        surface = surface + adj_field[0]
    members = ensemble.shape[0]
    block_rows = tile_lat // BLK
    block_cols = tile_lon // BLK
    own_blocks = block_rows * block_cols
    ens_blocks = ensemble.reshape(members, block_rows, BLK, block_cols, BLK)
    grad_blocks = surface.astype(jnp.bfloat16).reshape(block_rows, BLK, block_cols, BLK)
    local_coeffs = jnp.einsum(
        "mrpcq,rpcq->rcm", ens_blocks, grad_blocks, preferred_element_type=jnp.float32
    ).reshape(own_blocks, members)
    device_count = lon_count * lat_count
    total_blocks = own_blocks * device_count
    all_coeffs = lax.all_gather(local_coeffs, ("lon", "lat"), axis=0, tiled=True)
    partial_sums = jax.ops.segment_sum(
        taper[:, None] * all_coeffs[pair_src], pair_dst, num_segments=total_blocks
    )
    combined = lax.psum_scatter(partial_sums, ("lon", "lat"), scatter_dimension=0, tiled=True)
    combined16 = combined.astype(jnp.bfloat16).reshape(block_rows, block_cols, members)
    field_part = jnp.einsum(
        "mrpcq,rcm->rpcq", ens_blocks, combined16, preferred_element_type=jnp.float32
    ).reshape(tile_lat, tile_lon)
    prior_grad = var_scale * surface + field_part
    return (adj_field, prior_grad)


def solution(mesh):
    in_specs = (
        P(None, "lat", "lon"),
        P(None, "lat", "lon"),
        P("lat", "lon", None),
        P(None, "lat", "lon", None),
        P(),
        P(None, "lat", "lon"),
        P(("lon", "lat")),
        P(("lon", "lat")),
        P(("lon", "lat")),
        P("lat", "lon"),
    )
    out_specs = (P(None, "lat", "lon"), P("lat", "lon"))
    return jax.shard_map(
        per_device, mesh=mesh, in_specs=in_specs, out_specs=out_specs, check_vma=False
    )
```

profile of v0, /device:TPU:0, one launch (start us, length us, event | category | flops | bytes accessed | tf_op | source)
XLA Modules:
  0.0 1187.5 jit_solution(14152861951485718959)
XLA Ops:
  9.3 5.9 scatter_custom_fusion
  17.5 3.4 collective-permute-start
  20.9 3.6 collective-permute-start.1
  24.5 2.2 select_minimum_fusion
  29.0 3.1 fusion.74
  32.2 2.5 copy.20
  36.2 2.5 copy.24
  42.1 2.1 slice.205
  44.2 2.8 copy.22
  47.2 6.5 scatter_custom_fusion.1
  53.7 3.2 copy.23
  56.8 2.4 copy.21
  59.3 2.4 copy.25
  61.6 12.2 %fusion.4 = (f32[72,64,128]{2,1,0:T(8,128)S(1)}, f32[72,64,128]{2,1,0:T(8,128)}) fusion(f32[72,64,128]{2,1,0:T(8,128)} %copy-done.3, f32[72,1,128]{2,1,0:T(1,128)S(1)} %collective-permute-done, f32[72,1,128]{2,1,0:T(1,128)S(1)} %collective-permute-done.1, f32[72,66,1]{2,1,0:T(8,128)} %copy.25, f32[72,66,1]{2,1,0:T(8,128)} %copy.21, ...), kind=kLoop, calls=%fused_computation.20 | loop fusion | flops 16515072 | bytes 16692704 | tf_op jit(solution)/shard_map/add | solution.py:80
  73.9 4.0 collective-permute-start.6
  83.8 3.1 fusion.73
  87.0 2.5 copy.26
  91.5 2.5 copy.28
  94.1 6.1 scatter_custom_fusion.2
  100.2 2.4 copy.27
  102.6 2.4 copy.29
  105.0 10.6 fusion.37
  115.6 2.9 collective-permute-start.10
  118.6 2.8 collective-permute-start.11
  121.4 2.3 collective-permute-done.10
  124.5 3.1 fusion.72
  127.6 2.5 copy.30
  132.1 2.5 copy.32
  134.7 5.9 scatter_custom_fusion.3
  140.7 2.4 copy.31
  143.1 2.4 copy.33
  145.5 11.0 fusion.24
  156.5 4.1 collective-permute-start.14
  160.7 2.2 collective-permute-start.15
  162.9 2.0 collective-permute-done.14
  166.6 3.2 fusion.71
  169.7 3.2 copy.34
  174.8 3.1 copy.36
  177.9 6.1 scatter_custom_fusion.4
  184.0 2.3 copy.38
  186.3 3.1 copy.35
  189.4 3.2 copy.37
  192.6 10.8 fusion.11
  205.8 2.8 fusion.49
  208.9 302.3 %all-gather.2.cloned.1.call-done = f32[4096,64]{1,0:T(8,128)} async-done(((f32[32,64]{1,0:T(8,128)}), f32[4096,64]{1,0:T(8,128)}) %all-gather.2.cloned.1.call-update) | async-done | bytes 1048592 | tf_op jit(solution)/shard_map/all_gather | solution.py:99
  511.2 13.8 %scatter_custom_fusion.5 = f32[4096,64]{1,0:T(8,128)} fusion(s32[1024]{0:T(1024)} %param.17, f32[]{:T(128)} %constant.7.clone.1, f32[1024]{0:T(1024)S(1)} %copy-done.14, f32[4096,64]{1,0:T(8,128)} %all-gather.2.cloned.1.call-done, s32[1024]{0:T(1024)S(1)} %fusion.68), kind=kCustom, calls=%fused_computation.105 | custom fusion | flops 131072 | bytes 3154432 | tf_op jit(solution)/shard_map/scatter-add | solution.py:100
  525.0 648.7 %reduce-scatter.2.cloned.1.call-done = f32[32,64]{1,0:T(8,128)} async-done(((f32[4096,64]{1,0:T(8,128)}), f32[32,64]{1,0:T(8,128)}) %reduce-scatter.2.cloned.1.call-update) | async-done | bytes 8208 | tf_op jit(solution)/shard_map/reduce_scatter | solution.py:103
  1174.4 4.9 fusion.47
  (82 shorter events, 30.6 us)
Async XLA Ops:
  7.2 504.0 %all-gather.2.cloned.1.call-start = ((), (), s32[]{:S(2)}) async-start(), calls=%async_computation.1 | async-start | bytes 2113536 | tf_op jit(solution)/shard_map/all_gather | solution.py:99
  9.2 125.5 %copy-start.13 = (s32[1024,1]{0,1:T(1,128)}, s32[1024,1]{0,1:T(1,128)S(1)}, u32[]{:S(2)}) copy-start(s32[1024,1]{0,1:T(1,128)S(1)} %compare_select_fusion) | copy-start | bytes 12292
  16.1 1.4 copy-start.3
  17.5 11.0 collective-permute-start
  20.9 7.7 collective-permute-start.1
  24.5 4.1 copy-start.4
  26.7 35.0 %collective-permute-start.5 = (f32[72,1,128]{2,1,0:T(1,128)S(1)}, f32[72,1,128]{2,1,0:T(1,128)S(1)}, u32[]{:S(2)}, u32[]{:S(2)}) collective-permute-start(f32[72,1,128]{2,1,0:T(1,128)S(1)} %slice.208), channel_id=1, source_target_pairs={{0,1},{1,2},{2,3},{3,4},{4,5},{5,6},{6,7},{8,9},{9,10},{10,11},{11... | collective-permute-start | bytes 110600 | tf_op jit(solution)/shard_map/ppermute | solution.py:18
  34.7 22.1 %collective-permute-start.2 = (f32[72,66,1]{0,2,1:T(1,128)S(1)}, f32[72,66,1]{0,2,1:T(1,128)S(1)}, u32[]{:S(2)}, u32[]{:S(2)}) collective-permute-start(f32[72,66,1]{0,2,1:T(1,128)S(1)} %copy.20), channel_id=1, source_target_pairs={{8,0},{16,8},{24,16},{32,24},{40,32},{48,40},{56,48},{64,56},{72,6... | collective-permute-start | bytes 57032 | tf_op jit(solution)/shard_map/ppermute | solution.py:30
  38.7 20.5 %collective-permute-start.4 = (f32[72,66,1]{0,2,1:T(1,128)S(1)}, f32[72,66,1]{0,2,1:T(1,128)S(1)}, u32[]{:S(2)}, u32[]{:S(2)}) collective-permute-start(f32[72,66,1]{0,2,1:T(1,128)S(1)} %copy.24), channel_id=1, source_target_pairs={{0,8},{8,16},{16,24},{24,32},{32,40},{40,48},{48,56},{56,64},{64,7... | collective-permute-start | bytes 57032 | tf_op jit(solution)/shard_map/ppermute | solution.py:27
  40.7 1.4 copy-start.5
  47.0 6.6 collective-permute-start.3
  56.8 4.8 copy-start.10
  73.8 10.0 copy-start
  73.9 7.6 collective-permute-start.6
  77.9 5.5 collective-permute-start.7
  89.5 10.7 collective-permute-start.8
  94.0 8.6 collective-permute-start.9
  115.6 8.9 copy-start.1
  115.6 8.0 collective-permute-start.10
  118.6 5.5 collective-permute-start.11
  130.1 10.6 collective-permute-start.12
  134.7 8.4 collective-permute-start.13
  156.5 10.1 copy-start.2
  156.5 8.3 collective-permute-start.14
  160.7 5.5 collective-permute-start.15
  169.7 14.3 %copy-start.8 = (bf16[64,64,128]{2,1,0:T(8,128)(2,1)S(1)}, bf16[64,64,128]{2,1,0:T(8,128)(2,1)}, u32[]{:S(2)}) copy-start(bf16[64,64,128]{2,1,0:T(8,128)(2,1)} %param.15) | copy-start | bytes 3145732
  173.0 13.3 %collective-permute-start.16 = (f32[72,66,1]{0,2,1:T(1,128)}, f32[72,66,1]{0,2,1:T(1,128)}, u32[]{:S(2)}, u32[]{:S(2)}) collective-permute-start(f32[72,66,1]{0,2,1:T(1,128)} %copy.34), channel_id=1, source_target_pairs={{8,0},{16,8},{24,16},{32,24},{40,32},{48,40},{56,48},{64,56},{72,6... | collective-permute-start | bytes 57032 | tf_op jit(solution)/shard_map/ppermute | solution.py:30
  177.9 11.5 collective-permute-start.17
  186.3 6.3 copy-start.11
  203.4 1.4 copy-start.7
  204.8 4.1 copy-start.12
  204.8 306.4 %copy-start.14 = (f32[1024]{0:T(1024)S(1)}, f32[1024]{0:T(1024)}, u32[]{:S(2)}) copy-start(f32[1024]{0:T(1024)} %param.18) | copy-start | bytes 12292
  208.6 965.1 %reduce-scatter.2.cloned.1.call-start = ((), (), s32[]{:S(2)}) async-start(), calls=%async_computation.2 | async-start | bytes 2113536 | tf_op jit(solution)/shard_map/reduce_scatter | solution.py:103
  208.9 965.5 %copy-start.6 = (bf16[64,64,128]{0,2,1:T(8,128)(2,1)S(1)}, bf16[64,64,128]{0,2,1:T(8,128)(2,1)}, u32[]{:S(2)}) copy-start(bf16[64,64,128]{0,2,1:T(8,128)(2,1)} %copy.38) | copy-start | bytes 3145732
  525.0 654.6 %copy-start.9 = (f32[64,128]{1,0:T(8,128)S(1)}, f32[64,128]{1,0:T(8,128)}, u32[]{:S(2)}) copy-start(f32[64,128]{1,0:T(8,128)} %param.19) | copy-start | bytes 98308
Sparse Core Ops, SparseCore 0:
  208.7 302.4 all-gather.1
  525.1 648.5 reduce-scatter.1
where the time goes:
time: 1200 us; the launch traced here: 1190 us
  waiting for transfers between devices  961 us (80%)
  other arithmetic  98.3 us (8%)
  local copies, waits for them, and re-layouts  71.3 us (6%)
  starting transfers between devices  34.6 us (3%)
  between operations  14.9 us (1%)
    reduce_scatter x1, waiting for transfers between devices, per_device(): lax.psum_scatter(partial_sums, ('lon', 'lat'), scatter_dimension=0, tiled...  649 us
    all_gather x1, waiting for transfers between devices, per_device(): lax.all_gather(local_coeffs, ('lon', 'lat'), axis=0, tiled=True)  302 us
    add x4, other arithmetic, per_device(): adj_field + pos_east * (east_vals - adj_field)  44.5 us
    scatter-add x5, other arithmetic, forcing(): column = jnp.zeros((tile_lat * tile_lon,), jnp.float32).at[flat_cells].ad...  30.5 us
  transfers between devices with their start and end apart: 20, of which 8 were waited for; matrix products, arithmetic and copies ran while one was open for 6% of the time, Pallas kernels for 0%

commit v1 on v0

--- a/solution.py
+++ b/solution.py
@@ -2,8 +2,21 @@
 import jax.numpy as jnp
 from jax import lax
 from jax.sharding import PartitionSpec as P
+from jax.lax import all_to_all, psum
 
 BLK = 16
+
+
+def frame_raise(slab_in, row_dim):
+    return jnp.concatenate(
+        all_to_all(
+            jnp.stack(tuple((slab_in for _ in range(psum(1, ("lon", "lat"))))), axis=0),
+            ("lon", "lat"),
+            0,
+            0,
+        ),
+        axis=row_dim,
+    )
 
 
 def passed_along(block, axis, distance):
@@ -96,7 +109,7 @@
     ).reshape(own_blocks, members)
     device_count = lon_count * lat_count
     total_blocks = own_blocks * device_count
-    all_coeffs = lax.all_gather(local_coeffs, ("lon", "lat"), axis=0, tiled=True)
+    all_coeffs = frame_raise(local_coeffs, 0)
     partial_sums = jax.ops.segment_sum(
         taper[:, None] * all_coeffs[pair_src], pair_dst, num_segments=total_blocks
     )

time: 1200 us -> 923 us (0.77)
  waiting for transfers between devices: 961 us -> 671 us
    all_gather x1 -> x0, waiting for transfers between devices: 302 us -> none  [per_device(): lax.all_gather(local_coeffs, ('lon', 'lat'), axis=0, tiled=True)]
    all_to_all x0 -> x1, waiting for transfers between devices: none -> 17.8 us  [frame_raise(): all_to_all(jnp.stack(tuple((slab_in for _ in range(psum(1, ('lon', 'lat')...]
  transfers between devices with their start and end apart: 20 -> 20, of which waited for: 8 -> 8; matrix products, arithmetic and copies ran while one was open for 6% -> 7% of each run, Pallas kernels for 0% -> 0%
where the time goes in v1:
time: 923 us; the launch traced here: 915 us
  waiting for transfers between devices  671 us (73%)
  other arithmetic  101 us (11%)
  local copies, waits for them, and re-layouts  76.5 us (8%)
  starting transfers between devices  44.1 us (5%)
  between operations  14.6 us (2%)
    reduce_scatter x1, waiting for transfers between devices, per_device(): lax.psum_scatter(partial_sums, ('lon', 'lat'), scatter_dimension=0, tiled...  644 us
    add x4, other arithmetic, per_device(): adj_field + pos_east * (east_vals - adj_field)  44.4 us
    scatter-add x5, other arithmetic, forcing(): column = jnp.zeros((tile_lat * tile_lon,), jnp.float32).at[flat_cells].ad...  30.2 us
    slice x12, local copies, waits for them, and re-layouts, with_halo(): lax.slice_in_dim(block, 0, width, axis=dim)  23.6 us
  transfers between devices with their start and end apart: 20, of which 8 were waited for; matrix products, arithmetic and copies ran while one was open for 7% of the time, Pallas kernels for 0%

profile of v1, /device:TPU:0, one launch (start us, length us, event | category | flops | bytes accessed | tf_op | source)
XLA Modules:
  0.0 915.0 jit_solution(1015964062549016103)
XLA Ops:
  9.2 5.9 scatter_custom_fusion
  17.5 3.4 collective-permute-start
  20.9 3.6 collective-permute-start.1
  29.0 3.1 fusion.74
  32.1 2.5 copy.20
  36.2 2.5 copy.24
  44.2 2.8 copy.22
  47.2 6.1 scatter_custom_fusion.1
  53.3 3.2 copy.23
  56.5 2.4 copy.21
  58.9 2.4 copy.25
  61.3 12.2 %fusion.4 = (f32[72,64,128]{2,1,0:T(8,128)S(1)}, f32[72,64,128]{2,1,0:T(8,128)}) fusion(f32[72,64,128]{2,1,0:T(8,128)} %copy-done.3, f32[72,1,128]{2,1,0:T(1,128)S(1)} %collective-permute-done, f32[72,1,128]{2,1,0:T(1,128)S(1)} %collective-permute-done.1, f32[72,66,1]{2,1,0:T(8,128)} %copy.25, f32[72,66,1]{2,1,0:T(8,128)} %copy.21, ...), kind=kLoop, calls=%fused_computation.20 | loop fusion | flops 16515072 | bytes 16692704 | tf_op jit(solution)/shard_map/add | solution.py:93
  73.5 4.0 collective-permute-start.6
  83.5 3.1 fusion.73
  86.6 2.5 copy.26
  91.1 2.5 copy.28
  93.7 6.2 scatter_custom_fusion.2
  99.9 2.4 copy.27
  102.3 2.4 copy.29
  104.7 10.7 %fusion.37 = f32[72,64,128]{2,1,0:T(8,128)S(1)} fusion(f32[72,64,128]{2,1,0:T(8,128)} %copy-done, f32[72,1,128]{2,1,0:T(1,128)S(1)} %collective-permute-done.6, f32[72,1,128]{2,1,0:T(1,128)S(1)} %collective-permute-done.7, f32[72,64,128]{2,1,0:T(8,128)} %get-tuple-element.7, f32[72,66,1]{2,1,0:T(8,128)} %copy.29, f32[72,66,1]{2,1,0:T(8,128)} %copy.27, ...), kind=kLoop, calls=%fused_computation.70 | loop fusion | flops 15335424 | bytes 14300640 | tf_op jit(solution)/shard_map/add | solution.py:93
  115.4 2.9 collective-permute-start.10
  118.4 2.8 collective-permute-start.11
  121.2 2.3 collective-permute-done.10
  124.3 3.1 fusion.72
  127.4 2.5 copy.30
  131.9 2.5 copy.32
  134.5 5.9 scatter_custom_fusion.3
  140.5 2.4 copy.31
  142.9 2.4 copy.33
  145.3 10.9 %fusion.24 = f32[72,64,128]{2,1,0:T(8,128)S(1)} fusion(f32[72,64,128]{2,1,0:T(8,128)} %copy-done.1, f32[72,1,128]{2,1,0:T(1,128)S(1)} %collective-permute-done.10, f32[72,1,128]{2,1,0:T(1,128)S(1)} %collective-permute-done.11, f32[72,64,128]{2,1,0:T(8,128)} %get-tuple-element.7, f32[72,66,1]{2,1,0:T(8,128)} %copy.33, f32[72,66,1]{2,1,0:T(8,128)} %copy.31, ...), kind=kLoop, calls=%fused_computation.49 | loop fusion | flops 15335424 | bytes 14300640 | tf_op jit(solution)/shard_map/add | solution.py:93
  156.3 4.3 collective-permute-start.14
  160.6 2.2 collective-permute-start.15
  166.5 3.2 fusion.71
  169.7 3.2 copy.34
  174.7 3.1 copy.36
  177.8 6.1 scatter_custom_fusion.4
  183.9 2.3 copy.38
  186.2 3.1 copy.35
  189.3 3.2 copy.37
  192.5 10.7 %fusion.11 = f32[72,64,128]{2,1,0:T(8,128)S(1)} fusion(f32[72,64,128]{2,1,0:T(8,128)} %copy-done.2, f32[72,1,128]{2,1,0:T(1,128)S(1)} %collective-permute-done.14, f32[72,1,128]{2,1,0:T(1,128)S(1)} %collective-permute-done.15, f32[72,64,128]{2,1,0:T(8,128)} %get-tuple-element.7, f32[72,66,1]{2,1,0:T(8,128)} %copy.37, f32[72,66,1]{2,1,0:T(8,128)} %copy.35, ...), kind=kLoop, calls=%fused_computation.28 | loop fusion | flops 15335424 | bytes 14300640 | tf_op jit(solution)/shard_map/add | solution.py:93
  205.5 2.2 fusion.49
  208.0 2.3 reshape.164
  210.3 9.5 %all-to-all-start = ((f32[128,1,2048]{2,1,0:T(1,128)}), f32[128,1,2048]{2,1,0:T(1,128)S(1)}, u32[]{:S(2)}, u32[]{:S(2)}) async-start(f32[128,1,2048]{2,1,0:T(1,128)} %reshape.164), calls=%async_computation | async-start | bytes 2097152 | tf_op jit(solution)/shard_map/all_to_all | solution.py:12
  220.1 17.8 %all-to-all-done = f32[128,1,2048]{2,1,0:T(1,128)S(1)} async-done(((f32[128,1,2048]{2,1,0:T(1,128)}), f32[128,1,2048]{2,1,0:T(1,128)S(1)}, u32[]{:S(2)}, u32[]{:S(2)}) %all-to-all-start) | async-done | bytes 1048608 | tf_op jit(solution)/shard_map/all_to_all | solution.py:12
  238.3 3.1 reduce
  243.6 13.9 %scatter_custom_fusion.5 = f32[4096,64]{1,0:T(8,128)} fusion(s32[1024]{0:T(1024)} %param.17, f32[]{:T(128)} %constant.7.clone.1, f32[1024]{0:T(1024)S(1)} %copy-done.14, f32[4096,64]{1,0:T(8,128)} %bitcast.44, s32[1024]{0:T(1024)S(1)} %fusion.68), kind=kCustom, calls=%fused_computation.105 | custom fusion | flops 131072 | bytes 3154432 | tf_op jit(solution)/shard_map/scatter-add | solution.py:113
  257.6 643.8 %reduce-scatter.2.cloned.1.call-done = f32[32,64]{1,0:T(8,128)} async-done(((f32[4096,64]{1,0:T(8,128)}), f32[32,64]{1,0:T(8,128)}) %reduce-scatter.2.cloned.1.call-update) | async-done | bytes 8208 | tf_op jit(solution)/shard_map/reduce_scatter | solution.py:116
  902.1 4.9 fusion.47
  (86 shorter events, 39.7 us)
Async XLA Ops:
  9.2 125.3 %copy-start.13 = (s32[1024,1]{0,1:T(1,128)}, s32[1024,1]{0,1:T(1,128)S(1)}, u32[]{:S(2)}) copy-start(s32[1024,1]{0,1:T(1,128)S(1)} %compare_select_fusion) | copy-start | bytes 12292
  16.0 1.4 copy-start.3
  17.5 11.0 %collective-permute-start = (f32[72,1,128]{2,1,0:T(1,128)S(1)}, f32[72,1,128]{2,1,0:T(1,128)S(1)}, u32[]{:S(2)}, u32[]{:S(2)}) collective-permute-start(f32[72,1,128]{2,1,0:T(1,128)S(1)} %get-tuple-element.23), channel_id=1, source_target_pairs={{0,1},{1,2},{2,3},{3,4},{4,5},{5,6},{6,7},{7,0},{8,9},{9,10},{10,1... | collective-permute-start | bytes 110600 | tf_op jit(solution)/shard_map/ppermute | solution.py:40
  20.9 7.7 collective-permute-start.1
  24.4 4.1 copy-start.4
  26.6 34.6 %collective-permute-start.5 = (f32[72,1,128]{2,1,0:T(1,128)S(1)}, f32[72,1,128]{2,1,0:T(1,128)S(1)}, u32[]{:S(2)}, u32[]{:S(2)}) collective-permute-start(f32[72,1,128]{2,1,0:T(1,128)S(1)} %slice.208), channel_id=1, source_target_pairs={{0,1},{1,2},{2,3},{3,4},{4,5},{5,6},{6,7},{8,9},{9,10},{10,11},{11... | collective-permute-start | bytes 110600 | tf_op jit(solution)/shard_map/ppermute | solution.py:31
  34.7 21.8 %collective-permute-start.2 = (f32[72,66,1]{0,2,1:T(1,128)S(1)}, f32[72,66,1]{0,2,1:T(1,128)S(1)}, u32[]{:S(2)}, u32[]{:S(2)}) collective-permute-start(f32[72,66,1]{0,2,1:T(1,128)S(1)} %copy.20), channel_id=1, source_target_pairs={{8,0},{16,8},{24,16},{32,24},{40,32},{48,40},{56,48},{64,56},{72,6... | collective-permute-start | bytes 57032 | tf_op jit(solution)/shard_map/ppermute | solution.py:43
  38.7 20.2 %collective-permute-start.4 = (f32[72,66,1]{0,2,1:T(1,128)S(1)}, f32[72,66,1]{0,2,1:T(1,128)S(1)}, u32[]{:S(2)}, u32[]{:S(2)}) collective-permute-start(f32[72,66,1]{0,2,1:T(1,128)S(1)} %copy.24), channel_id=1, source_target_pairs={{0,8},{8,16},{16,24},{24,32},{32,40},{40,48},{48,56},{56,64},{64,7... | collective-permute-start | bytes 57032 | tf_op jit(solution)/shard_map/ppermute | solution.py:40
  40.7 1.4 copy-start.5
  47.0 6.3 collective-permute-start.3
  56.5 4.8 copy-start.10
  73.5 10.0 %copy-start = (f32[72,64,128]{2,1,0:T(8,128)}, f32[72,64,128]{2,1,0:T(8,128)S(1)}, u32[]{:S(2)}) copy-start(f32[72,64,128]{2,1,0:T(8,128)S(1)} %get-tuple-element.6) | copy-start | bytes 7077892
  73.5 7.6 collective-permute-start.6
  77.6 5.5 collective-permute-start.7
  89.1 10.8 %collective-permute-start.8 = (f32[72,66,1]{0,2,1:T(1,128)S(1)}, f32[72,66,1]{0,2,1:T(1,128)S(1)}, u32[]{:S(2)}, u32[]{:S(2)}) collective-permute-start(f32[72,66,1]{0,2,1:T(1,128)S(1)} %copy.26), channel_id=1, source_target_pairs={{8,0},{16,8},{24,16},{32,24},{40,32},{48,40},{56,48},{64,56},{72,6... | collective-permute-start | bytes 57032 | tf_op jit(solution)/shard_map/ppermute | solution.py:43
  93.7 8.7 collective-permute-start.9
  115.4 8.9 copy-start.1
  115.4 8.0 collective-permute-start.10
  118.4 5.5 collective-permute-start.11
  129.9 10.6 %collective-permute-start.12 = (f32[72,66,1]{0,2,1:T(1,128)S(1)}, f32[72,66,1]{0,2,1:T(1,128)S(1)}, u32[]{:S(2)}, u32[]{:S(2)}) collective-permute-start(f32[72,66,1]{0,2,1:T(1,128)S(1)} %copy.30), channel_id=1, source_target_pairs={{8,0},{16,8},{24,16},{32,24},{40,32},{48,40},{56,48},{64,56},{72,6... | collective-permute-start | bytes 57032 | tf_op jit(solution)/shard_map/ppermute | solution.py:43
  134.5 8.4 collective-permute-start.13
  156.2 10.3 %copy-start.2 = (f32[72,64,128]{2,1,0:T(8,128)}, f32[72,64,128]{2,1,0:T(8,128)S(1)}, u32[]{:S(2)}) copy-start(f32[72,64,128]{2,1,0:T(8,128)S(1)} %fusion.24) | copy-start | bytes 7077892
  156.3 8.5 collective-permute-start.14
  160.6 5.5 collective-permute-start.15
  169.7 14.3 %copy-start.8 = (bf16[64,64,128]{2,1,0:T(8,128)(2,1)S(1)}, bf16[64,64,128]{2,1,0:T(8,128)(2,1)}, u32[]{:S(2)}) copy-start(bf16[64,64,128]{2,1,0:T(8,128)(2,1)} %param.15) | copy-start | bytes 3145732
  172.9 13.3 %collective-permute-start.16 = (f32[72,66,1]{0,2,1:T(1,128)}, f32[72,66,1]{0,2,1:T(1,128)}, u32[]{:S(2)}, u32[]{:S(2)}) collective-permute-start(f32[72,66,1]{0,2,1:T(1,128)} %copy.34), channel_id=1, source_target_pairs={{8,0},{16,8},{24,16},{32,24},{40,32},{48,40},{56,48},{64,56},{72,6... | collective-permute-start | bytes 57032 | tf_op jit(solution)/shard_map/ppermute | solution.py:43
  177.8 11.5 %collective-permute-start.17 = (f32[72,66,1]{0,2,1:T(1,128)}, f32[72,66,1]{0,2,1:T(1,128)}, u32[]{:S(2)}, u32[]{:S(2)}) collective-permute-start(f32[72,66,1]{0,2,1:T(1,128)} %copy.36), channel_id=1, source_target_pairs={{0,8},{8,16},{16,24},{24,32},{32,40},{40,48},{48,56},{56,64},{64,7... | collective-permute-start | bytes 57032 | tf_op jit(solution)/shard_map/ppermute | solution.py:40
  186.2 6.3 copy-start.11
  203.2 1.4 copy-start.7
  208.0 12.1 %copy-start.12 = (s32[1024]{0:T(1024)S(1)}, s32[1024]{0:T(1024)}, u32[]{:S(2)}) copy-start(s32[1024]{0:T(1024)} %param.16) | copy-start | bytes 12292
  210.3 27.5 %all-to-all-start = ((f32[128,1,2048]{2,1,0:T(1,128)}), f32[128,1,2048]{2,1,0:T(1,128)S(1)}, u32[]{:S(2)}, u32[]{:S(2)}) async-start(f32[128,1,2048]{2,1,0:T(1,128)} %reshape.164), calls=%async_computation | async-start | bytes 2097152 | tf_op jit(solution)/shard_map/all_to_all | solution.py:12
  219.8 681.6 %reduce-scatter.2.cloned.1.call-start = ((), (), s32[]{:S(2)}) async-start(), calls=%async_computation.2 | async-start | bytes 2113536 | tf_op jit(solution)/shard_map/reduce_scatter | solution.py:116
  238.3 5.3 copy-start.14
  243.6 658.5 %copy-start.6 = (bf16[64,64,128]{0,2,1:T(8,128)(2,1)S(1)}, bf16[64,64,128]{0,2,1:T(8,128)(2,1)}, u32[]{:S(2)}) copy-start(bf16[64,64,128]{0,2,1:T(8,128)(2,1)} %copy.38) | copy-start | bytes 3145732
  257.6 649.7 %copy-start.9 = (f32[64,128]{1,0:T(8,128)S(1)}, f32[64,128]{1,0:T(8,128)}, u32[]{:S(2)}) copy-start(f32[64,128]{1,0:T(8,128)} %param.19) | copy-start | bytes 98308
Sparse Core Ops, SparseCore 0:
  257.7 643.6 reduce-scatter.1
